TPU v7x, 32 devices: a whole 2x2x4 slice. The times are simulated.
32 devices in a mesh: row: 4 (over z), col: 8 (over y, x, core).
Axes of the slice: x: 2, y: 2, z: 4, core: 2. Of those that a mesh axis runs over, the one named last changes fastest.
Arguments:
- weight: float32 [16384, 16384], P('row', 'col'), may hold values from -0.046875 to 0.046875
- leak: float32 [16384], P('col'), may hold values from 0.1 to 1
- rates: float32 [3, 256, 16384], P(None, 'row', 'col'), may hold values from -0.95 to 0.95
- cotangent: float32 [256, 16384], P('row', 'col'), may hold values from -2 to 2
Outputs:
- grad_input: float32 [256, 16384], P('row', 'col')
- grad_weight: float32 [16384, 16384], P('row', 'col')
- grad_noise: float32 [3, 16384], P(None, 'row')
All inputs are finite; a program needn't handle non-finite values.
Results may differ from a plain program's by a relative error of at most 0.0001.
Values sent between devices are 32-bit elements; how exact they have to be, the bound alone decides.
A program may use at most 192 MiB of HBM per device.

v0:
```python
import jax
import jax.numpy as jnp
from jax import lax
from jax.sharding import PartitionSpec as P

TSTEPS = 3


def shards(weight, leak, rates, cotangent):
    n_col = lax.axis_size("col")
    own_rows = cotangent.shape[0]
    local_units = cotangent.shape[1]
    full_rates = lax.all_gather(rates, "row", axis=1, tiled=True)
    grad_weight = jnp.zeros(weight.shape, jnp.float32)
    noise_list = []
    carried = cotangent
    for step_back in range(TSTEPS - 1, -1, -1):
        scaled = leak[None, :] * carried
        spread = scaled.reshape(own_rows, local_units // n_col, n_col)
        by_col = lax.all_to_all(spread, "col", split_axis=2, concat_axis=1, tiled=True)
        by_row = lax.all_to_all(by_col, "row", split_axis=1, concat_axis=0, tiled=True)
        gathered = lax.all_gather(by_row, "col", axis=2, tiled=True)
        unit_block = gathered.reshape(gathered.shape[0], gathered.shape[1] * gathered.shape[2])
        rates_now = full_rates[step_back]
        noise_list.insert(0, jnp.sum(unit_block, axis=0))
        grad_weight = grad_weight + lax.dot_general(
            unit_block,
            rates_now,
            (((0,), (0,)), ((), ())),
            precision=lax.Precision.HIGHEST,
            preferred_element_type=jnp.float32,
        )
        partial_sum = jnp.dot(
            unit_block, weight, precision=lax.Precision.HIGHEST, preferred_element_type=jnp.float32
        )
        adjoint = lax.psum_scatter(partial_sum, "row", scatter_dimension=0, tiled=True)
        local_rates = rates[step_back]
        carried = (1.0 - leak[None, :]) * carried + (1.0 - local_rates * local_rates) * adjoint
    return (carried, grad_weight, jnp.stack(noise_list))


def solution(mesh):
    placed = (P("row", "col"), P("col"), P(None, "row", "col"), P("row", "col"))
    return jax.shard_map(
        shards,
        mesh=mesh,
        in_specs=placed,
        out_specs=(P("row", "col"), P("row", "col"), P(None, "row")),
        check_vma=False,
    )
```

profile of v0, /device:TPU:0, one launch (start us, length us, event | category | flops | bytes accessed | tf_op | source)
XLA Modules:
  0.0 633.9 jit_solution(5892808969612367369)
XLA Ops:
  7.2 1.1 broadcast_multiply_fusion.2
  9.0 14.7 %all_to_all.108 = f32[64,256,8]{1,0,2:T(8,128)S(1)} all-to-all(f32[64,256,8]{1,0,2:T(8,128)S(1)} %copy.20), channel_id=1, replica_groups=mesh['row'=4,'col'=8] {'col'}, dimensions={2} | all-to-all | bytes 1048576 | tf_op jit(solution)/shard_map/all_to_all | solution.py:20
  24.1 0.5 broadcast.24
  24.6 9.3 %reduce.3 = f32[2048,64]{1,0:T(8,128)S(1)} reduce(f32[2048,1,64]{2,1,0:T(1,128)S(1)} %bitcast.75, f32[]{:T(128)} %broadcast.24), dimensions={1}, to_apply=%bitcast.64.reduce_sub_computation | reduce | bytes 1048580
  33.9 0.7 reshape.48
  34.6 18.6 %all_to_all.109 = f32[4,1,32768]{2,1,0:T(1,128)S(1)} all-to-all(f32[4,1,32768]{2,1,0:T(1,128)S(1)} %reshape.48), channel_id=1, replica_groups=mesh['row'=4,'col'=8] {'row'}, dimensions={0} | all-to-all | bytes 1048576 | tf_op jit(solution)/shard_map/all_to_all | solution.py:21
  53.2 2.1 reduce.4
  55.3 1.3 reshape.49
  57.0 1.0 copy.24
  58.0 0.6 reduce-scatter.4.cloned.1.call-start
  58.6 34.0 %all-gather.5.cloned.1.call-done = f32[256,512,8]{1,0,2:T(8,128)} async-done(((f32[256,512,1]{1,0,2:T(8,128)}), f32[256,512,8]{1,0,2:T(8,128)}) %all-gather.5.cloned.1.call-update) | async-done | bytes 4194320 | tf_op jit(solution)/shard_map/all_gather | solution.py:22
  92.6 5.4 copy.25
  98.0 33.8 %fusion.9 = f32[256,2048]{1,0:T(8,128)} fusion(f32[4096,2048]{1,0:T(8,128)} %param.4, f32[256,512,8]{0,2,1:T(8,128)} %copy.25), kind=kOutput, calls=%fused_computation.10 | convolution fusion | flops 25769803776 | bytes 39845888 | tf_op jit(solution)/shard_map/dot_general | solution.py:33
  132.0 43.7 %reduce-scatter.4.cloned.1.call-done = f32[64,2048]{1,0:T(8,128)} async-done(((f32[256,2048]{1,0:T(8,128)}), f32[64,2048]{1,0:T(8,128)}) %reduce-scatter.4.cloned.1.call-update) | async-done | bytes 524304 | tf_op jit(solution)/shard_map/reduce_scatter | solution.py:36
  175.7 1.3 broadcast_multiply_fusion.1
  177.7 13.3 %all_to_all.110 = f32[64,256,8]{1,0,2:T(8,128)S(1)} all-to-all(f32[64,256,8]{1,0,2:T(8,128)S(1)} %copy.27), channel_id=1, replica_groups=mesh['row'=4,'col'=8] {'col'}, dimensions={2} | all-to-all | bytes 1048576 | tf_op jit(solution)/shard_map/all_to_all | solution.py:20
  191.4 9.3 %reduce.5 = f32[2048,64]{1,0:T(8,128)S(1)} reduce(f32[2048,1,64]{2,1,0:T(1,128)S(1)} %bitcast.76, f32[]{:T(128)} %broadcast.24), dimensions={1}, to_apply=%bitcast.66.reduce_sub_computation | reduce | bytes 1048580
  200.8 0.7 reshape.50
  201.4 16.6 %all_to_all.111 = f32[4,1,32768]{2,1,0:T(1,128)S(1)} all-to-all(f32[4,1,32768]{2,1,0:T(1,128)S(1)} %reshape.50), channel_id=1, replica_groups=mesh['row'=4,'col'=8] {'row'}, dimensions={0} | all-to-all | bytes 1048576 | tf_op jit(solution)/shard_map/all_to_all | solution.py:21
  218.0 2.1 reduce.6
  220.2 1.3 reshape.51
  221.8 1.0 copy.31
  223.1 34.3 %all-gather.7.cloned.1.call-done = f32[256,512,8]{1,0,2:T(8,128)} async-done(((f32[256,512,1]{1,0,2:T(8,128)}), f32[256,512,8]{1,0,2:T(8,128)}) %all-gather.7.cloned.1.call-update) | async-done | bytes 4194320 | tf_op jit(solution)/shard_map/all_gather | solution.py:22
  257.4 5.5 copy.32
  262.9 33.8 %fusion.5 = f32[256,2048]{1,0:T(8,128)} fusion(f32[4096,2048]{1,0:T(8,128)} %param.4, f32[256,512,8]{0,2,1:T(8,128)} %copy.32), kind=kOutput, calls=%fused_computation.6 | convolution fusion | flops 25769803776 | bytes 39845888 | tf_op jit(solution)/shard_map/dot_general | solution.py:33
  296.8 0.5 all-gather.11.cloned.1.call-update
  297.4 43.2 %reduce-scatter.6.cloned.1.call-done = f32[64,2048]{1,0:T(8,128)} async-done(((f32[256,2048]{1,0:T(8,128)}), f32[64,2048]{1,0:T(8,128)}) %reduce-scatter.6.cloned.1.call-update) | async-done | bytes 524304 | tf_op jit(solution)/shard_map/reduce_scatter | solution.py:36
  340.6 2.0 broadcast_multiply_fusion
  343.3 13.5 %all_to_all.112 = f32[64,256,8]{1,0,2:T(8,128)} all-to-all(f32[64,256,8]{1,0,2:T(8,128)S(1)} %copy.34), channel_id=1, replica_groups=mesh['row'=4,'col'=8] {'col'}, dimensions={2} | all-to-all | bytes 1048576 | tf_op jit(solution)/shard_map/all_to_all | solution.py:20
  356.9 1.4 copy.47
  358.2 10.3 %reduce.7 = f32[2048,64]{1,0:T(8,128)} reduce(f32[2048,1,64]{2,1,0:T(1,128)S(1)} %bitcast.77, f32[]{:T(128)} %broadcast.24), dimensions={1}, to_apply=%bitcast.68.reduce_sub_computation | reduce | bytes 1048580
  368.6 1.9 reshape.52
  370.4 31.9 %all_to_all.113 = f32[4,1,32768]{2,1,0:T(1,128)S(1)} all-to-all(f32[4,1,32768]{2,1,0:T(1,128)S(1)} %reshape.52), channel_id=1, replica_groups=mesh['row'=4,'col'=8] {'row'}, dimensions={0} | all-to-all | bytes 1048576 | tf_op jit(solution)/shard_map/all_to_all | solution.py:21
  402.4 2.1 reduce.8
  404.5 1.3 reshape.53
  406.2 1.0 copy.38
  407.2 0.5 reduce-scatter.8.cloned.1.call-start
  407.7 2.6 reduce_sum.29
  410.6 57.0 %all-gather.11.cloned.1.call-done = f32[3,256,2048]{2,1,0:T(8,128)} async-done(((f32[3,64,2048]{2,1,0:T(8,128)}), f32[3,256,2048]{2,1,0:T(8,128)}) %all-gather.11.cloned.1.call-update) | async-done | bytes 6291472 | tf_op jit(solution)/shard_map/all_gather | solution.py:13
  467.6 32.4 %fusion.7 = f32[4096,2048]{1,0:T(8,128)} fusion(f32[256,512,8]{0,2,1:T(8,128)} %copy.25, f32[3,256,2048]{2,1,0:T(8,128)} %all-gather.11.cloned.1.call-done), kind=kOutput, calls=%fused_computation.8 | convolution fusion | flops 25769803776 | bytes 39845888 | tf_op jit(solution)/shard_map/dot_general | solution.py:26
  500.0 2.7 reduce_sum.28
  503.0 32.4 %fusion.3 = f32[4096,2048]{1,0:T(8,128)} fusion(f32[256,512,8]{0,2,1:T(8,128)} %copy.32, f32[3,256,2048]{2,1,0:T(8,128)} %all-gather.11.cloned.1.call-done), kind=kOutput, calls=%fused_computation.4 | convolution fusion | flops 25769803776 | bytes 39845888 | tf_op jit(solution)/shard_map/dot_general | solution.py:26
  535.4 2.6 reduce_sum.27
  538.3 5.5 copy.39
  543.8 34.0 %fusion.1 = f32[256,2048]{1,0:T(8,128)} fusion(f32[4096,2048]{1,0:T(8,128)} %param.4, f32[256,512,8]{0,2,1:T(8,128)} %copy.39), kind=kOutput, calls=%fused_computation.2 | convolution fusion | flops 25769803776 | bytes 39845888 | tf_op jit(solution)/shard_map/dot_general | solution.py:33
  577.8 0.7 pad_maximum_fusion
  578.5 46.4 %add_add_fusion = f32[4096,2048]{1,0:T(8,128)} fusion(f32[4096,2048]{1,0:T(8,128)} %fusion.7, f32[4096,2048]{1,0:T(8,128)} %fusion.3, f32[256,512,8]{0,2,1:T(8,128)} %copy.39, f32[3,256,2048]{2,1,0:T(8,128)} %all-gather.11.cloned.1.call-done), kind=kOutput, calls=%fused_computation | convolution fusion | flops 25786580992 | bytes 106954752 | tf_op jit(solution)/shard_map/dot_general | solution.py:26
  624.9 1.9 fusion.11
  (41 shorter events, 5.3 us)
Async XLA Ops:
  7.2 85.4 %all-gather.5.cloned.1.call-start = ((), (), s32[]{:S(2)}) async-start(), calls=%async_computation.9 | async-start | bytes 4718592 | tf_op jit(solution)/shard_map/all_gather | solution.py:22
  58.0 117.7 %reduce-scatter.4.cloned.1.call-start = ((), (), s32[]{:S(2)}) async-start(), calls=%async_computation.10 | async-start | bytes 2621440 | tf_op jit(solution)/shard_map/reduce_scatter | solution.py:36
  98.0 33.9 %copy-start.4 = (f32[2048]{0:T(1024)S(1)}, f32[2048]{0:T(1024)}, u32[]{:S(2)}) copy-start(f32[2048]{0:T(1024)} %param.5) | copy-start | bytes 24580
  98.0 77.7 %copy-start.1 = (f32[64,2048]{1,0:T(8,128)S(1)}, f32[64,2048]{1,0:T(8,128)}, u32[]{:S(2)}) copy-start(f32[64,2048]{1,0:T(8,128)} %param.7) | copy-start | bytes 1572868
  131.9 125.5 %all-gather.7.cloned.1.call-start = ((), (), s32[]{:S(2)}) async-start(), calls=%async_computation.11 | async-start | bytes 4718592 | tf_op jit(solution)/shard_map/all_gather | solution.py:22
  222.8 117.7 %reduce-scatter.6.cloned.1.call-start = ((), (), s32[]{:S(2)}) async-start(), calls=%async_computation.12 | async-start | bytes 2621440 | tf_op jit(solution)/shard_map/reduce_scatter | solution.py:36
  262.9 77.7 %copy-start.3 = (f32[64,2048]{1,0:T(8,128)S(1)}, f32[64,2048]{1,0:T(8,128)}, u32[]{:S(2)}) copy-start(f32[64,2048]{1,0:T(8,128)} %reduce-scatter.4.cloned.1.call-done) | copy-start | bytes 1572868
  296.7 43.8 %copy-start = (f32[3,64,2048]{2,1,0:T(8,128)S(1)}, f32[3,64,2048]{2,1,0:T(8,128)}, u32[]{:S(2)}) copy-start(f32[3,64,2048]{2,1,0:T(8,128)} %param.6) | copy-start | bytes 4718596
  296.8 170.9 %all-gather.11.cloned.1.call-start = ((), (), s32[]{:S(2)}) async-start(), calls=%async_computation.15 | async-start | bytes 7864320 | tf_op jit(solution)/shard_map/all_gather | solution.py:13
  297.4 238.0 %all-gather.9.cloned.1.call-start = ((), (), s32[]{:S(2)}) async-start(), calls=%async_computation.13 | async-start | bytes 4718592 | tf_op jit(solution)/shard_map/all_gather | solution.py:22
  407.2 217.7 %reduce-scatter.8.cloned.1.call-start = ((), (), s32[]{:S(2)}) async-start(), calls=%async_computation.14 | async-start | bytes 2621440 | tf_op jit(solution)/shard_map/reduce_scatter | solution.py:36
  578.5 46.4 %copy-start.2 = (f32[64,2048]{1,0:T(8,128)S(1)}, f32[64,2048]{1,0:T(8,128)}, u32[]{:S(2)}) copy-start(f32[64,2048]{1,0:T(8,128)} %get-tuple-element.4) | copy-start | bytes 1572868
Sparse Core Ops, SparseCore 0:
  58.1 34.4 all-gather.4
  132.0 43.6 reduce-scatter.3
  222.9 34.4 all-gather.6
  296.9 43.6 reduce-scatter.5
  342.0 125.6 all-gather.10
  469.4 34.7 all-gather.8
  577.9 41.7 reduce-scatter.7
where the time goes:
time: 642 us; the launch traced here: 634 us
  waiting for transfers between devices  213 us (33%)
  matrix products  213 us (33%)
  blocking collectives  109 us (17%)
  other arithmetic  50.4 us (8%)
  local copies, waits for them, and re-layouts  33 us (5%)
  between operations  14.7 us (2%)
    dot_general x3, matrix products, shards(): lax.dot_general(unit_block, rates_now, (((0,), (0,)), ((), ())), precisio...  111 us
    dot_general x3, matrix products, shards(): jnp.dot(unit_block, weight, precision=lax.Precision.HIGHEST, preferred_el...  102 us
    reduce_scatter x3, waiting for transfers between devices, shards(): lax.psum_scatter(partial_sum, 'row', scatter_dimension=0, tiled=True)  86.9 us
    all_gather x3, waiting for transfers between devices, shards(): gathered = lax.all_gather(by_row, 'col', axis=2, tiled=True)  68.3 us
    all_to_all x3, blocking collectives, shards(): lax.all_to_all(by_col, 'row', split_axis=1, concat_axis=0, tiled=True)  67.2 us
    all_gather x1, waiting for transfers between devices, shards(): full_rates = lax.all_gather(rates, 'row', axis=1, tiled=True)  57 us
    all_to_all x3, blocking collectives, shards(): lax.all_to_all(spread, 'col', split_axis=2, concat_axis=1, tiled=True)  41.6 us
    unnamed x3, other arithmetic  29 us
  transfers between devices with their start and end apart: 7, of which 5 were waited for; matrix products, arithmetic and copies ran while one was open for 22% of the time, Pallas kernels for 0%

commit v1 on v0

--- a/solution.py
+++ b/solution.py
@@ -4,9 +4,62 @@
 from jax.sharding import PartitionSpec as P
 
 TSTEPS = 3
+SUBLANES = 8
+PREC = lax.Precision.HIGH
 
 
-def shards(weight, leak, rates, cotangent):
+def spread_units(scaled, n_row, n_col):
+    own_rows, local_units = scaled.shape
+    block = own_rows // n_col
+    per_row = n_col // n_row
+    by_col = lax.all_to_all(
+        scaled.reshape(n_col, block, local_units), "col", split_axis=0, concat_axis=0, tiled=True
+    )
+    by_row = lax.all_to_all(by_col, "row", split_axis=0, concat_axis=0, tiled=True)
+    piece = by_row.reshape(n_row, per_row, block, local_units)
+    piece = piece.transpose(0, 2, 1, 3).reshape(n_row * block, per_row * local_units)
+    return lax.all_gather(piece, "col", axis=0, tiled=True)
+
+
+def shards_blocks(weight, leak, rates, cotangent):
+    n_col = lax.axis_size("col")
+    n_row = lax.axis_size("row")
+    own_rows, local_units = cotangent.shape
+    block = own_rows // n_col
+    trials = own_rows * n_row
+
+    def ordered(x):
+        y = x.reshape(x.shape[0], n_row, n_col, block, local_units)
+        return y.transpose(0, 2, 1, 3, 4).reshape(x.shape[0], trials, local_units)
+
+    full_rates = ordered(lax.all_gather(rates, "row", axis=1, tiled=True))
+    noise_list = []
+    carried = cotangent
+    blocks = []
+    for step_back in range(TSTEPS - 1, -1, -1):
+        scaled = leak[None, :] * carried
+        unit_block = spread_units(scaled, n_row, n_col)
+        blocks.append(unit_block)
+        noise_list.insert(0, jnp.sum(unit_block, axis=0))
+        partial_sum = jnp.dot(unit_block, weight, precision=PREC, preferred_element_type=jnp.float32)
+        partial_sum = partial_sum.reshape(n_col, n_row, block, local_units)
+        partial_sum = partial_sum.transpose(1, 0, 2, 3).reshape(trials, local_units)
+        adjoint = lax.psum_scatter(partial_sum, "row", scatter_dimension=0, tiled=True)
+        local_rates = rates[step_back]
+        carried = (1.0 - leak[None, :]) * carried + (1.0 - local_rates * local_rates) * adjoint
+    dims = (((0,), (0,)), ((), ()))
+    early = lax.dot_general(
+        jnp.concatenate(blocks[:-1], axis=0),
+        jnp.concatenate([full_rates[s] for s in range(TSTEPS - 1, 0, -1)], axis=0),
+        dims, precision=PREC, preferred_element_type=jnp.float32,
+    )
+    grad_weight = early + lax.dot_general(
+        blocks[-1], full_rates[0], dims, precision=PREC, preferred_element_type=jnp.float32
+    )
+    return (carried, grad_weight, jnp.stack(noise_list))
+
+
+def shards_any(weight, leak, rates, cotangent):
     n_col = lax.axis_size("col")
     own_rows = cotangent.shape[0]
     local_units = cotangent.shape[1]
@@ -24,15 +77,10 @@
         rates_now = full_rates[step_back]
         noise_list.insert(0, jnp.sum(unit_block, axis=0))
         grad_weight = grad_weight + lax.dot_general(
-            unit_block,
-            rates_now,
-            (((0,), (0,)), ((), ())),
-            precision=lax.Precision.HIGHEST,
-            preferred_element_type=jnp.float32,
+            unit_block, rates_now, (((0,), (0,)), ((), ())),
+            precision=PREC, preferred_element_type=jnp.float32,
         )
-        partial_sum = jnp.dot(
-            unit_block, weight, precision=lax.Precision.HIGHEST, preferred_element_type=jnp.float32
-        )
+        partial_sum = jnp.dot(unit_block, weight, precision=PREC, preferred_element_type=jnp.float32)
         adjoint = lax.psum_scatter(partial_sum, "row", scatter_dimension=0, tiled=True)
         local_rates = rates[step_back]
         carried = (1.0 - leak[None, :]) * carried + (1.0 - local_rates * local_rates) * adjoint
@@ -40,6 +88,13 @@
 
 
 def solution(mesh):
+    n_row, n_col = mesh.shape["row"], mesh.shape["col"]
+
+    def shards(weight, leak, rates, cotangent):
+        fits = cotangent.shape[0] % (n_col * SUBLANES) == 0 and n_col % n_row == 0
+        body = shards_blocks if fits else shards_any
+        return body(weight, leak, rates, cotangent)
+
     placed = (P("row", "col"), P("col"), P(None, "row", "col"), P("row", "col"))
     return jax.shard_map(
         shards,

time: 642 us -> 541 us (0.84); the launches traced: 634 us -> 541 us
  matrix products: 213 us -> 127 us
  waiting for transfers between devices: 213 us -> 260 us
  other arithmetic: 50.4 us -> 13.9 us
  local copies, waits for them, and re-layouts: 33 us -> 15.5 us
    dot_general x6 -> x5, matrix products: 213 us -> 127 us  [the longest x3 61.4 us: shards_blocks(): jnp.dot(unit_block, weight, precision=PREC, preferred_element_type=jnp.fl...]
    all_gather x4, waiting for transfers between devices: 125 us -> 173 us  [the longest x3 95.3 us: spread_units(): return lax.all_gather(piece, 'col', axis=0, tiled=True)]
    unnamed x3 -> x0, other arithmetic: 29 us -> none
    all_gather x3 -> x0, local copies, waits for them, and re-layouts: 16.4 us -> none  [shards(): gathered = lax.all_gather(by_row, 'col', axis=2, tiled=True)]
    transpose x0 -> x3, local copies, waits for them, and re-layouts: none -> 7.82 us  [shards_blocks(): partial_sum = partial_sum.transpose(1, 0, 2, 3).reshape(trials, local_units)]
    slice x0 -> x4, local copies, waits for them, and re-layouts: none -> 7.69 us  [the longest x2 4.77 us: shards_blocks(): full_rates[0]]
    unnamed x17 -> x6, local copies, waits for them, and re-layouts: 7.58 us -> 0.02 us
    all_to_all x3 -> x0, other arithmetic: 6.42 us -> none  [shards(): lax.all_to_all(by_col, 'row', split_axis=1, concat_axis=0, tiled=True)]
  transfers between devices with their start and end apart: 7 -> 7, of which waited for: 5 -> 6; matrix products, arithmetic and copies ran while one was open for 22% -> 15% of each run, Pallas kernels for 0% -> 0%
where the time goes in v1:
time: 541 us
  waiting for transfers between devices  260 us (48%)
  matrix products  127 us (23%)
  blocking collectives  109 us (20%)
  local copies, waits for them, and re-layouts  15.5 us (3%)
  between operations  14.2 us (3%)
  other arithmetic  13.9 us (3%)
    all_gather x3, waiting for transfers between devices, spread_units(): return lax.all_gather(piece, 'col', axis=0, tiled=True)  95.3 us
    reduce_scatter x3, waiting for transfers between devices, shards_blocks(): lax.psum_scatter(partial_sum, 'row', scatter_dimension=0, tiled=True)  86.9 us
    all_gather x1, waiting for transfers between devices, shards_blocks(): full_rates = ordered(lax.all_gather(rates, 'row', axis=1, tiled=True))  77.6 us
    all_to_all x3, blocking collectives, spread_units(): lax.all_to_all(by_col, 'row', split_axis=0, concat_axis=0, tiled=True)  68.4 us
    dot_general x3, matrix products, shards_blocks(): jnp.dot(unit_block, weight, precision=PREC, preferred_element_type=jnp.fl...  61.4 us
    all_to_all x3, blocking collectives, spread_units(): lax.all_to_all(scaled.reshape(n_col, block, local_units), 'col', split_ax...  41 us
    dot_general x1, matrix products, shards_blocks(): lax.dot_general(jnp.concatenate(blocks[:-1], axis=0), jnp.concatenate([fu...  33.7 us
    dot_general x1, matrix products, shards_blocks(): lax.dot_general(blocks[-1], full_rates[0], dims, precision=PREC, preferre...  31.9 us
  transfers between devices with their start and end apart: 7, of which 6 were waited for; matrix products, arithmetic and copies ran while one was open for 15% of the time, Pallas kernels for 0%

profile of v1, /device:TPU:0, one launch (start us, length us, event | category | flops | bytes accessed | tf_op | source)
XLA Modules:
  0.0 540.6 jit_solution(13712195354255252632)
XLA Ops:
  7.2 0.0 all-gather.5.cloned.1.call-start
  7.2 1.1 multiply_bitcast_fusion.2
  8.3 14.7 %all_to_all.30 = f32[8,8,2048]{2,1,0:T(8,128)S(1)} all-to-all(f32[8,8,2048]{2,1,0:T(8,128)S(1)} %multiply_bitcast_fusion.2), channel_id=1, replica_groups=mesh['row'=4,'col'=8] {'col'}, dimensions={0} | all-to-all | bytes 1048576 | tf_op jit(solution)/shard_map/all_to_all | solution.py:15
  23.0 18.7 %all_to_all.31 = f32[8,8,2048]{2,1,0:T(8,128)} all-to-all(f32[8,8,2048]{2,1,0:T(8,128)S(1)} %all_to_all.30), channel_id=1, replica_groups=mesh['row'=4,'col'=8] {'row'}, dimensions={0} | all-to-all | bytes 1048576 | tf_op jit(solution)/shard_map/all_to_all | solution.py:18
  41.7 0.0 all-gather.5.cloned.1.call-update
  41.7 0.0 reduce-scatter.4.cloned.1.call-start
  41.8 34.5 %all-gather.5.cloned.1.call-done = f32[256,4096]{1,0:T(8,128)} async-done(((f32[32,4096]{1,0:T(8,128)}), f32[256,4096]{1,0:T(8,128)}) %all-gather.5.cloned.1.call-update) | async-done | bytes 4194320 | tf_op jit(solution)/shard_map/all_gather | solution.py:21
  76.3 20.2 %fusion.13 = f32[256,2048]{1,0:T(8,128)S(1)} fusion(f32[256,4096]{1,0:T(8,128)} %all-gather.5.cloned.1.call-done, f32[4096,2048]{1,0:T(8,128)} %param.4), kind=kOutput, calls=%fused_computation.21 | convolution fusion | flops 12884901888 | bytes 39845888 | tf_op jit(solution)/shard_map/dot_general | solution.py:44
  96.5 0.0 copy-start.2
  96.5 0.0 copy-start.1
  96.6 1.5 copy.19
  98.0 0.0 reduce-scatter.4.cloned.1.call-update
  98.0 0.0 all-gather.7.cloned.1.call-start
  98.1 43.7 %reduce-scatter.4.cloned.1.call-done = f32[64,2048]{1,0:T(8,128)} async-done(((f32[256,2048]{1,0:T(8,128)}), f32[64,2048]{1,0:T(8,128)}) %reduce-scatter.4.cloned.1.call-update) | async-done | bytes 524304 | tf_op jit(solution)/shard_map/reduce_scatter | solution.py:47
  141.8 1.3 multiply_bitcast_fusion.1
  143.2 13.2 %all_to_all.32 = f32[8,8,2048]{2,1,0:T(8,128)S(1)} all-to-all(f32[8,8,2048]{2,1,0:T(8,128)S(1)} %multiply_bitcast_fusion.1), channel_id=1, replica_groups=mesh['row'=4,'col'=8] {'col'}, dimensions={0} | all-to-all | bytes 1048576 | tf_op jit(solution)/shard_map/all_to_all | solution.py:15
  156.3 17.3 %all_to_all.33 = f32[8,8,2048]{2,1,0:T(8,128)} all-to-all(f32[8,8,2048]{2,1,0:T(8,128)S(1)} %all_to_all.32), channel_id=1, replica_groups=mesh['row'=4,'col'=8] {'row'}, dimensions={0} | all-to-all | bytes 1048576 | tf_op jit(solution)/shard_map/all_to_all | solution.py:18
  173.6 0.0 all-gather.7.cloned.1.call-update
  173.6 0.0 reduce-scatter.6.cloned.1.call-start
  173.7 34.5 %all-gather.7.cloned.1.call-done = f32[256,4096]{1,0:T(8,128)} async-done(((f32[32,4096]{1,0:T(8,128)}), f32[256,4096]{1,0:T(8,128)}) %all-gather.7.cloned.1.call-update) | async-done | bytes 4194320 | tf_op jit(solution)/shard_map/all_gather | solution.py:21
  208.2 20.6 %fusion.14 = f32[256,2048]{1,0:T(8,128)} fusion(f32[256,4096]{1,0:T(8,128)} %all-gather.7.cloned.1.call-done, f32[4096,2048]{1,0:T(8,128)} %param.4), kind=kOutput, calls=%fused_computation.22 | convolution fusion | flops 12884901888 | bytes 39845888 | tf_op jit(solution)/shard_map/dot_general | solution.py:44
  228.8 3.2 copy.20
  232.1 0.0 reduce-scatter.6.cloned.1.call-update
  232.1 0.0 all-gather.11.cloned.1.call-start
  232.1 0.5 all-gather.11.cloned.1.call-update
  232.7 0.0 all-gather.9.cloned.1.call-start
  232.7 43.2 %reduce-scatter.6.cloned.1.call-done = f32[64,2048]{1,0:T(8,128)} async-done(((f32[256,2048]{1,0:T(8,128)}), f32[64,2048]{1,0:T(8,128)}) %reduce-scatter.6.cloned.1.call-update) | async-done | bytes 524304 | tf_op jit(solution)/shard_map/reduce_scatter | solution.py:47
  275.9 1.4 multiply_bitcast_fusion
  277.3 13.2 %all_to_all.34 = f32[8,8,2048]{2,1,0:T(8,128)S(1)} all-to-all(f32[8,8,2048]{2,1,0:T(8,128)S(1)} %get-tuple-element.3), channel_id=1, replica_groups=mesh['row'=4,'col'=8] {'col'}, dimensions={0} | all-to-all | bytes 1048576 | tf_op jit(solution)/shard_map/all_to_all | solution.py:15
  290.4 32.4 %all_to_all.35 = f32[8,8,2048]{2,1,0:T(8,128)} all-to-all(f32[8,8,2048]{2,1,0:T(8,128)S(1)} %all_to_all.34), channel_id=1, replica_groups=mesh['row'=4,'col'=8] {'row'}, dimensions={0} | all-to-all | bytes 1048576 | tf_op jit(solution)/shard_map/all_to_all | solution.py:18
  322.8 0.0 all-gather.9.cloned.1.call-update
  322.8 0.0 reduce-scatter.8.cloned.1.call-start
  322.9 2.5 reduce_sum.29
  325.4 77.6 %all-gather.11.cloned.1.call-done = f32[3,256,2048]{2,1,0:T(8,128)} async-done(((f32[3,64,2048]{2,1,0:T(8,128)}), f32[3,256,2048]{2,1,0:T(8,128)}) %all-gather.11.cloned.1.call-update) | async-done | bytes 6291472 | tf_op jit(solution)/shard_map/all_gather | solution.py:35
  403.0 3.3 fusion.12
  406.2 1.5 copy.23
  407.7 1.4 copy.22
  409.2 1.5 copy.24
  410.6 2.5 reduce_sum.28
  413.2 26.2 %all-gather.9.cloned.1.call-done = f32[256,4096]{1,0:T(8,128)} async-done(((f32[32,4096]{1,0:T(8,128)}), f32[256,4096]{1,0:T(8,128)}) %all-gather.9.cloned.1.call-update) | async-done | bytes 4194320 | tf_op jit(solution)/shard_map/all_gather | solution.py:21
  439.4 20.6 %fusion.15 = f32[256,2048]{1,0:T(8,128)} fusion(f32[256,4096]{1,0:T(8,128)} %all-gather.9.cloned.1.call-done, f32[4096,2048]{1,0:T(8,128)} %param.4), kind=kOutput, calls=%fused_computation.23 | convolution fusion | flops 12884901888 | bytes 39845888 | tf_op jit(solution)/shard_map/dot_general | solution.py:44
  460.0 3.1 copy.21
  463.1 0.0 reduce-scatter.8.cloned.1.call-update
  463.2 33.7 %fusion = f32[4096,2048]{1,0:T(8,128)} fusion(f32[256,4096]{1,0:T(8,128)} %all-gather.7.cloned.1.call-done, f32[256,4096]{1,0:T(8,128)} %all-gather.5.cloned.1.call-done, f32[256,2048]{1,0:T(8,128)} %bitcast.76, f32[256,2048]{1,0:T(8,128)} %bitcast.77), kind=kOutput, calls=%fused_computation.1 | convolution fusion | flops 25772949504 | bytes 46137344 | tf_op jit(solution)/shard_map/dot_general | solution.py:51
  496.9 2.4 reduce_sum.27
  499.3 0.7 pad_maximum_fusion
  500.0 31.9 %convolution_add_fusion = f32[4096,2048]{1,0:T(8,128)} fusion(f32[4096,2048]{1,0:T(8,128)} %fusion, f32[256,4096]{1,0:T(8,128)} %all-gather.9.cloned.1.call-done, f32[256,2048]{1,0:T(8,128)} %bitcast.74), kind=kOutput, calls=%fused_computation | convolution fusion | flops 12893290496 | bytes 73400320 | tf_op jit(solution)/shard_map/dot_general | solution.py:56
  531.9 1.9 fusion.7
  (6 shorter events, 0.0 us)
Async XLA Ops:
  7.2 69.1 %all-gather.5.cloned.1.call-start = ((), (), s32[]{:S(2)}) async-start(), calls=%async_computation.9 | async-start | bytes 4718592 | tf_op jit(solution)/shard_map/all_gather | solution.py:21
  41.7 100.1 %reduce-scatter.4.cloned.1.call-start = ((), (), s32[]{:S(2)}) async-start(), calls=%async_computation.10 | async-start | bytes 2621440 | tf_op jit(solution)/shard_map/reduce_scatter | solution.py:47
  96.5 1.6 copy-start.2
  96.5 45.3 %copy-start.1 = (f32[64,2048]{1,0:T(8,128)S(1)}, f32[64,2048]{1,0:T(8,128)}, u32[]{:S(2)}) copy-start(f32[64,2048]{1,0:T(8,128)} %param.7) | copy-start | bytes 1572868
  98.0 110.2 %all-gather.7.cloned.1.call-start = ((), (), s32[]{:S(2)}) async-start(), calls=%async_computation.11 | async-start | bytes 4718592 | tf_op jit(solution)/shard_map/all_gather | solution.py:21
  173.6 102.2 %reduce-scatter.6.cloned.1.call-start = ((), (), s32[]{:S(2)}) async-start(), calls=%async_computation.12 | async-start | bytes 2621440 | tf_op jit(solution)/shard_map/reduce_scatter | solution.py:47
  228.8 47.1 %copy-start = (f32[3,64,2048]{2,1,0:T(8,128)S(1)}, f32[3,64,2048]{2,1,0:T(8,128)}, u32[]{:S(2)}) copy-start(f32[3,64,2048]{2,1,0:T(8,128)} %param.6) | copy-start | bytes 4718596
  232.1 170.9 %all-gather.11.cloned.1.call-start = ((), (), s32[]{:S(2)}) async-start(), calls=%async_computation.15 | async-start | bytes 7864320 | tf_op jit(solution)/shard_map/all_gather | solution.py:35
  232.7 206.8 %all-gather.9.cloned.1.call-start = ((), (), s32[]{:S(2)}) async-start(), calls=%async_computation.13 | async-start | bytes 4718592 | tf_op jit(solution)/shard_map/all_gather | solution.py:21
  322.8 209.0 %reduce-scatter.8.cloned.1.call-start = ((), (), s32[]{:S(2)}) async-start(), calls=%async_computation.14 | async-start | bytes 2621440 | tf_op jit(solution)/shard_map/reduce_scatter | solution.py:47
Sparse Core Ops, SparseCore 0:
  41.9 34.4 all-gather.4
  98.2 43.6 reduce-scatter.3
  173.8 34.4 all-gather.6
  232.2 43.6 reduce-scatter.5
  277.3 125.6 all-gather.10
  404.7 34.6 all-gather.8
  463.3 43.6 reduce-scatter.7

commit v2 on v1

v2 whole, which is shorter than its diff:
```python
import functools

import jax
import jax.numpy as jnp
from jax import lax
from jax.experimental import pallas as pl
from jax.experimental.pallas import tpu as pltpu
from jax.sharding import PartitionSpec as P

TSTEPS = 3
SUBLANES = 8
CORES = 2
MESH = pl.DeviceIdType.MESH
PREC = lax.Precision.HIGH


def spread_kernel(n_row, n_col, x_ref, out_ref, by_col, by_row, a_send, a_recv, b_send, b_recv,
                  c_send, c_recv, p_send, p_recv, own_sem, f_send, f_recv, keep_sem):
    r, c = lax.axis_index("row"), lax.axis_index("col")
    per_row = n_col // n_row
    n_chip = n_col // CORES
    chip, core = c // CORES, lax.rem(c, CORES)
    partner = chip * CORES + (CORES - 1 - core)

    def remote(src, dst, send, recv, row, col):
        return pltpu.make_async_remote_copy(
            src_ref=src, dst_ref=dst, send_sem=send, recv_sem=recv,
            device_id=(row, col), device_id_type=MESH,
        )

    barrier = pltpu.get_barrier_semaphore()
    for d in range(1, n_col):
        pl.semaphore_signal(barrier, inc=1, device_id=(r, lax.rem(c + d, n_col)), device_id_type=MESH)
    for e in range(1, n_row):
        pl.semaphore_signal(barrier, inc=1, device_id=(lax.rem(r + e, n_row), c), device_id_type=MESH)
    pl.semaphore_wait(barrier, n_col + n_row - 2)

    keep = pltpu.make_async_copy(x_ref.at[c], by_col.at[c], keep_sem)
    keep.start()
    sends = []
    for d in range(1, n_col):
        to = lax.rem(c + d, n_col)
        copy = remote(x_ref.at[to], by_col.at[c], a_send.at[d], a_recv.at[d], r, to)
        copy.start()
        sends.append(copy)
    keep.wait()
    for d in range(1, n_col):
        sends[d - 1].wait_recv()

    def part(k):
        return by_col.at[pl.ds(k * per_row, per_row)]

    for e in range(1, n_row):
        to = lax.rem(r + e, n_row)
        copy = remote(part(to), by_row.at[r], b_send.at[e], b_recv.at[e], to, c)
        copy.start()
        sends.append(copy)

    arrived = []
    local = []
    relays = []

    def relay(e):
        origin = lax.rem(r - e + n_row, n_row)
        for d in range(1, n_chip):
            arrived[e][d - 1].wait_recv()
            source = lax.rem(chip - d + n_chip, n_chip) * CORES + core
            slot = out_ref.at[origin, source]
            copy = remote(slot, slot, f_send.at[e, d], f_recv.at[e, d], r, partner)
            copy.start()
            relays.append(copy)

    for e in range(n_row):
        origin = lax.rem(r - e + n_row, n_row)
        if e == 0:
            piece = part(r)
        else:
            piece = by_row.at[origin]
            remote(part(origin), piece, b_send.at[e], b_recv.at[e], origin, c).wait_recv()
        slot = out_ref.at[origin, c]
        mine = []
        for d in range(1, n_chip):
            to = lax.rem(chip + d, n_chip) * CORES + core
            copy = remote(piece, slot, c_send.at[e, d], c_recv.at[e, d], r, to)
            copy.start()
            mine.append(copy)
        arrived.append(mine)
        copy = remote(piece, slot, p_send.at[e], p_recv.at[e], r, partner)
        copy.start()
        relays.append(copy)
        own = pltpu.make_async_copy(piece, slot, own_sem.at[e])
        own.start()
        local.append(own)
        if e > 0:
            relay(e - 1)
    relay(n_row - 1)
    for copy in sends:
        copy.wait_send()
    for mine in arrived:
        for copy in mine:
            copy.wait_send()
    for copy in relays:
        copy.wait_send()
        copy.wait_recv()
    for own in local:
        own.wait()


def spread_units(scaled, n_row, n_col):
    own_rows, units = scaled.shape
    block = own_rows // n_col
    per_row = n_col // n_row
    n_chip = n_col // CORES
    dma = pltpu.SemaphoreType.DMA
    out = pl.pallas_call(
        functools.partial(spread_kernel, n_row, n_col),
        out_shape=jax.ShapeDtypeStruct((n_row, n_col, per_row, block, units), jnp.float32),
        in_specs=[pl.BlockSpec(memory_space=pltpu.VMEM)],
        out_specs=pl.BlockSpec(memory_space=pl.ANY),
        scratch_shapes=[
            pltpu.VMEM((n_col, block, units), jnp.float32),
            pltpu.VMEM((n_row, per_row, block, units), jnp.float32),
            dma((n_col,)), dma((n_col,)),
            dma((n_row,)), dma((n_row,)),
            dma((n_row, n_chip)), dma((n_row, n_chip)),
            dma((n_row,)), dma((n_row,)), dma((n_row,)),
            dma((n_row, n_chip)), dma((n_row, n_chip)),
            dma,
        ],
        compiler_params=pltpu.CompilerParams(collective_id=0, has_side_effects=True),
        name="spread",
    )(scaled.reshape(n_col, block, units))
    return out.transpose(0, 1, 3, 2, 4).reshape(n_row * own_rows, per_row * units)


def shards_blocks(weight, leak, rates, cotangent):
    n_col = lax.axis_size("col")
    n_row = lax.axis_size("row")
    noise_list = []
    carried = cotangent
    grad_weight = None
    for step_back in range(TSTEPS - 1, -1, -1):
        scaled = leak[None, :] * carried
        scaled, own_rates = lax.optimization_barrier((scaled, rates[step_back]))
        rates_now = lax.all_gather(own_rates, "row", axis=0, tiled=True)
        unit_block = spread_units(scaled, n_row, n_col)
        noise_list.insert(0, jnp.sum(unit_block, axis=0))
        partial_sum = jnp.dot(unit_block, weight, precision=PREC, preferred_element_type=jnp.float32)
        partial_sum, rates_now = lax.optimization_barrier((partial_sum, rates_now))
        adjoint = lax.psum_scatter(partial_sum, "row", scatter_dimension=0, tiled=True)
        product = lax.dot_general(
            unit_block, rates_now, (((0,), (0,)), ((), ())),
            precision=PREC, preferred_element_type=jnp.float32,
        )
        grad_weight = product if grad_weight is None else grad_weight + product
        if step_back > 0:
            adjoint, grad_weight = lax.optimization_barrier((adjoint, grad_weight))
        carried = (1.0 - leak[None, :]) * carried + (1.0 - own_rates * own_rates) * adjoint
    return (carried, grad_weight, jnp.stack(noise_list))


def shards_any(weight, leak, rates, cotangent):
    n_col = lax.axis_size("col")
    own_rows = cotangent.shape[0]
    local_units = cotangent.shape[1]
    full_rates = lax.all_gather(rates, "row", axis=1, tiled=True)
    grad_weight = jnp.zeros(weight.shape, jnp.float32)
    noise_list = []
    carried = cotangent
    for step_back in range(TSTEPS - 1, -1, -1):
        scaled = leak[None, :] * carried
        spread = scaled.reshape(own_rows, local_units // n_col, n_col)
        by_col = lax.all_to_all(spread, "col", split_axis=2, concat_axis=1, tiled=True)
        by_row = lax.all_to_all(by_col, "row", split_axis=1, concat_axis=0, tiled=True)
        gathered = lax.all_gather(by_row, "col", axis=2, tiled=True)
        unit_block = gathered.reshape(gathered.shape[0], gathered.shape[1] * gathered.shape[2])
        rates_now = full_rates[step_back]
        noise_list.insert(0, jnp.sum(unit_block, axis=0))
        grad_weight = grad_weight + lax.dot_general(
            unit_block, rates_now, (((0,), (0,)), ((), ())),
            precision=PREC, preferred_element_type=jnp.float32,
        )
        partial_sum = jnp.dot(unit_block, weight, precision=PREC, preferred_element_type=jnp.float32)
        adjoint = lax.psum_scatter(partial_sum, "row", scatter_dimension=0, tiled=True)
        local_rates = rates[step_back]
        carried = (1.0 - leak[None, :]) * carried + (1.0 - local_rates * local_rates) * adjoint
    return (carried, grad_weight, jnp.stack(noise_list))


def solution(mesh):
    n_row, n_col = mesh.shape["row"], mesh.shape["col"]

    def shards(weight, leak, rates, cotangent):
        fits = cotangent.shape[0] % (n_col * SUBLANES) == 0 and n_col % n_row == 0 and n_col % CORES == 0
        body = shards_blocks if fits else shards_any
        return body(weight, leak, rates, cotangent)

    placed = (P("row", "col"), P("col"), P(None, "row", "col"), P("row", "col"))
    return jax.shard_map(
        shards,
        mesh=mesh,
        in_specs=placed,
        out_specs=(P("row", "col"), P("row", "col"), P(None, "row")),
        check_vma=False,
    )
```

time: 541 us -> 380 us (0.70)
  waiting for transfers between devices: 260 us -> 66 us
  Pallas kernels: 0 us -> 134 us
  blocking collectives: 109 us -> 0 us
  matrix products: 127 us -> 148 us
  local copies, waits for them, and re-layouts: 15.5 us -> 4.57 us
    all_gather x4 -> x3, waiting for transfers between devices: 173 us -> 0.01 us  [shards_blocks(): rates_now = lax.all_gather(own_rates, 'row', axis=0, tiled=True)]
    pallas_call x0 -> x3, Pallas kernels: none -> 134 us  [spread_units(): pl.pallas_call(functools.partial(spread_kernel, n_row, n_col), out_shape=...]
    all_to_all x6 -> x0, blocking collectives: 109 us -> none  [the longest x3 68.4 us: spread_units(): lax.all_to_all(by_col, 'row', split_axis=0, concat_axis=0, tiled=True)]
    reduce_scatter x3, waiting for transfers between devices: 86.9 us -> 65.9 us  [shards_blocks(): lax.psum_scatter(partial_sum, 'row', scatter_dimension=0, tiled=True)]
    dot_general x2 -> x3, matrix products: 65.6 us -> 86.1 us  [shards_blocks(): lax.dot_general(unit_block, rates_now, (((0,), (0,)), ((), ())), precisio...]
    transpose x3 -> x0, local copies, waits for them, and re-layouts: 7.82 us -> none  [shards_blocks(): partial_sum = partial_sum.transpose(1, 0, 2, 3).reshape(trials, local_units)]
    slice x4 -> x0, local copies, waits for them, and re-layouts: 7.69 us -> none  [the longest x2 4.77 us: shards_blocks(): full_rates[0]]
    mul x0 -> x3, other arithmetic: none -> 5.87 us  [shards_blocks(): scaled = leak[None, :] * carried]
  transfers between devices with their start and end apart: 7 -> 6, of which waited for: 6 -> 3; matrix products, arithmetic and copies ran while one was open for 15% -> 40% of each run, Pallas kernels for 0% -> 35%
where the time goes in v2:
time: 380 us; the launch traced here: 379 us
  matrix products  148 us (39%)
  Pallas kernels  134 us (35%)
  waiting for transfers between devices  66 us (17%)
  between operations  14.2 us (4%)
  other arithmetic  11.5 us (3%)
  local copies, waits for them, and re-layouts  4.57 us (1%)
    pallas_call x3, Pallas kernels, spread_units(): pl.pallas_call(functools.partial(spread_kernel, n_row, n_col), out_shape=...  134 us
    dot_general x3, matrix products, shards_blocks(): lax.dot_general(unit_block, rates_now, (((0,), (0,)), ((), ())), precisio...  86.1 us
    reduce_scatter x3, waiting for transfers between devices, shards_blocks(): lax.psum_scatter(partial_sum, 'row', scatter_dimension=0, tiled=True)  65.9 us
    dot_general x3, matrix products, shards_blocks(): jnp.dot(unit_block, weight, precision=PREC, preferred_element_type=jnp.fl...  62 us
  transfers between devices with their start and end apart: 6, of which 3 were waited for; matrix products, arithmetic and copies ran while one was open for 40% of the time, Pallas kernels for 35%

profile of v2, /device:TPU:0, one launch (start us, length us, event | category | flops | bytes accessed | tf_op | source)
XLA Modules:
  0.0 379.4 jit_solution(4342491744552462314)
XLA Ops:
  7.2 0.0 all-gather.4.cloned.1.call-start
  7.2 2.6 slice_bitcast_fusion
  9.8 1.9 broadcast_multiply_fusion.2
  11.7 0.0 all-gather.4.cloned.1.call-update
  11.7 0.0 reduce-scatter.4.cloned.1.call-start
  11.8 46.8 %spread.3 = f32[4,8,2,8,2048]{4,3,2,1,0:T(8,128)} custom-call(f32[8,8,2048]{2,1,0:T(8,128)} %bitcast.49), custom_call_target="tpu_custom_call" | custom-call | tf_op jit(solution)/shard_map/spread/pallas_call | solution.py:115
  58.6 0.0 copy-start.7
  58.6 20.7 %fusion = f32[256,2048]{1,0:T(8,128)} fusion(f32[256,4096]{1,0:T(8,128)} %bitcast.46, f32[4096,2048]{1,0:T(8,128)} %param.4), kind=kOutput, calls=%fused_computation.16 | convolution fusion | flops 12884901888 | bytes 39845888 | tf_op jit(solution)/shard_map/dot_general | solution.py:148
  79.3 0.0 reduce-scatter.4.cloned.1.call-update
  79.3 0.0 all-gather.6.cloned.1.call-start
  79.4 0.0 copy-done.7
  79.4 0.0 copy-start.2
  79.4 0.0 copy-start.3
  79.4 22.3 %fusion.1 = f32[4096,2048]{1,0:T(8,128)} fusion(f32[256,4096]{1,0:T(8,128)} %bitcast.47, f32[256,2048]{1,0:T(8,128)} %all-gather.4.cloned.1.call-done), kind=kOutput, calls=%fused_computation.17 | convolution fusion | flops 12884901888 | bytes 39845888 | tf_op jit(solution)/shard_map/dot_general | solution.py:151
  101.7 29.9 %reduce-scatter.4.cloned.1.call-done = f32[64,2048]{1,0:T(8,128)} async-done(((f32[256,2048]{1,0:T(8,128)}), f32[64,2048]{1,0:T(8,128)}) %reduce-scatter.4.cloned.1.call-update) | async-done | bytes 524304 | tf_op jit(solution)/shard_map/reduce_scatter | solution.py:150
  131.7 0.0 copy-done.2
  131.7 0.0 copy-done.3
  131.7 1.9 broadcast_multiply_fusion.1
  133.6 0.0 all-gather.6.cloned.1.call-update
  133.7 0.2 reduce-scatter.6.cloned.1.call-start
  133.9 43.8 %spread.4 = f32[4,8,2,8,2048]{4,3,2,1,0:T(8,128)} custom-call(f32[8,8,2048]{2,1,0:T(8,128)} %bitcast.50), custom_call_target="tpu_custom_call" | custom-call | tf_op jit(solution)/shard_map/spread/pallas_call | solution.py:115
  177.7 20.7 %fusion.2 = f32[256,2048]{1,0:T(8,128)} fusion(f32[256,4096]{1,0:T(8,128)} %bitcast.42, f32[4096,2048]{1,0:T(8,128)} %param.4), kind=kOutput, calls=%fused_computation.18 | convolution fusion | flops 12884901888 | bytes 39845888 | tf_op jit(solution)/shard_map/dot_general | solution.py:148
  198.3 0.0 reduce-scatter.6.cloned.1.call-update
  198.3 0.0 copy-start.4
  198.4 0.0 copy-start.6
  198.4 0.0 all-gather.8.cloned.1.call-start
  198.4 31.9 %convolution_add_fusion.1 = f32[4096,2048]{1,0:T(8,128)} fusion(f32[4096,2048]{1,0:T(8,128)} %fusion.1, f32[256,4096]{1,0:T(8,128)} %bitcast.43, f32[256,2048]{1,0:T(8,128)} %all-gather.6.cloned.1.call-done), kind=kOutput, calls=%fused_computation.1 | convolution fusion | flops 12893290496 | bytes 73400320 | tf_op jit(solution)/shard_map/dot_general | solution.py:151
  230.3 20.8 %reduce-scatter.6.cloned.1.call-done = f32[64,2048]{1,0:T(8,128)} async-done(((f32[256,2048]{1,0:T(8,128)}), f32[64,2048]{1,0:T(8,128)}) %reduce-scatter.6.cloned.1.call-update) | async-done | bytes 524304 | tf_op jit(solution)/shard_map/reduce_scatter | solution.py:150
  251.1 0.0 copy-done.4
  251.1 0.0 copy-done.6
  251.1 2.0 broadcast_multiply_fusion
  253.1 0.0 all-gather.8.cloned.1.call-update
  253.2 0.3 reduce-scatter.8.cloned.1.call-start
  253.4 43.9 %spread.5 = f32[4,8,2,8,2048]{4,3,2,1,0:T(8,128)} custom-call(f32[8,8,2048]{2,1,0:T(8,128)} %bitcast.48), custom_call_target="tpu_custom_call" | custom-call | tf_op jit(solution)/shard_map/spread/pallas_call | solution.py:115
  297.3 20.6 %fusion.3 = f32[256,2048]{1,0:T(8,128)} fusion(f32[256,4096]{1,0:T(8,128)} %bitcast.44, f32[4096,2048]{1,0:T(8,128)} %param.4), kind=kOutput, calls=%fused_computation.19 | convolution fusion | flops 12884901888 | bytes 39845888 | tf_op jit(solution)/shard_map/dot_general | solution.py:148
  317.9 0.0 reduce-scatter.8.cloned.1.call-update
  318.0 0.0 copy-start
  318.0 0.0 copy-start.1
  318.0 2.6 bitcast_reduce_fusion.2
  320.6 0.8 copy-done
  321.4 0.2 bitcast_reduce_fusion.1
  321.7 1.0 copy-done.1
  322.7 0.2 bitcast_reduce_fusion
  322.9 0.7 pad_maximum_fusion
  323.6 31.8 %convolution_add_fusion = f32[4096,2048]{1,0:T(8,128)} fusion(f32[4096,2048]{1,0:T(8,128)} %convolution_add_fusion.1, f32[256,4096]{1,0:T(8,128)} %bitcast.45, f32[256,2048]{1,0:T(8,128)} %all-gather.8.cloned.1.call-done), kind=kOutput, calls=%fused_computation | convolution fusion | flops 12893290496 | bytes 73400320 | tf_op jit(solution)/shard_map/dot_general | solution.py:151
  355.5 15.2 %reduce-scatter.8.cloned.1.call-done = f32[64,2048]{1,0:T(8,128)} async-done(((f32[256,2048]{1,0:T(8,128)}), f32[64,2048]{1,0:T(8,128)}) %reduce-scatter.8.cloned.1.call-update) | async-done | bytes 524304 | tf_op jit(solution)/shard_map/reduce_scatter | solution.py:150
  370.6 0.0 copy-done.5
  370.6 1.9 multiply_add_fusion
  (8 shorter events, 0.1 us)
Async XLA Ops:
  7.2 72.1 %all-gather.4.cloned.1.call-start = ((), (), s32[]{:S(2)}) async-start(), calls=%async_computation.3 | async-start | bytes 2621440 | tf_op jit(solution)/shard_map/all_gather | solution.py:145
  11.7 119.9 %reduce-scatter.4.cloned.1.call-start = ((), (), s32[]{:S(2)}) async-start(), calls=%async_computation.4 | async-start | bytes 2621440 | tf_op jit(solution)/shard_map/reduce_scatter | solution.py:150
  58.6 20.8 %copy-start.7 = (f32[2048]{0:T(1024)S(1)}, f32[2048]{0:T(1024)}, u32[]{:S(2)}) copy-start(f32[2048]{0:T(1024)} %param.5) | copy-start | bytes 24580
  79.3 119.0 %all-gather.6.cloned.1.call-start = ((), (), s32[]{:S(2)}) async-start(), calls=%async_computation.5 | async-start | bytes 2621440 | tf_op jit(solution)/shard_map/all_gather | solution.py:145
  79.4 52.3 %copy-start.2 = (f32[64,2048]{1,0:T(8,128)S(1)}, f32[64,2048]{1,0:T(8,128)}, u32[]{:S(2)}) copy-start(f32[64,2048]{1,0:T(8,128)} %get-tuple-element.19) | copy-start | bytes 1572868
  79.4 52.3 %copy-start.3 = (f32[64,2048]{1,0:T(8,128)S(1)}, f32[64,2048]{1,0:T(8,128)}, u32[]{:S(2)}) copy-start(f32[64,2048]{1,0:T(8,128)} %param.7) | copy-start | bytes 1572868
  133.7 117.4 %reduce-scatter.6.cloned.1.call-start = ((), (), s32[]{:S(2)}) async-start(), calls=%async_computation.6 | async-start | bytes 2621440 | tf_op jit(solution)/shard_map/reduce_scatter | solution.py:150
  198.3 52.7 %copy-start.4 = (f32[64,2048]{1,0:T(8,128)S(1)}, f32[64,2048]{1,0:T(8,128)}, u32[]{:S(2)}) copy-start(f32[64,2048]{1,0:T(8,128)} %get-tuple-element.24) | copy-start | bytes 1572868
  198.4 52.7 %copy-start.6 = (f32[64,2048]{1,0:T(8,128)S(1)}, f32[64,2048]{1,0:T(8,128)}, u32[]{:S(2)}) copy-start(f32[64,2048]{1,0:T(8,128)} %reduce-scatter.4.cloned.1.call-done) | copy-start | bytes 1572868
  198.4 119.6 %all-gather.8.cloned.1.call-start = ((), (), s32[]{:S(2)}) async-start(), calls=%async_computation.7 | async-start | bytes 2621440 | tf_op jit(solution)/shard_map/all_gather | solution.py:145
  253.2 117.5 %reduce-scatter.8.cloned.1.call-start = ((), (), s32[]{:S(2)}) async-start(), calls=%async_computation.8 | async-start | bytes 2621440 | tf_op jit(solution)/shard_map/reduce_scatter | solution.py:150
  318.0 3.5 copy-start
  318.0 4.7 %copy-start.1 = (f32[4,8,2,8,2048]{4,3,2,1,0:T(8,128)S(1)}, f32[4,8,2,8,2048]{4,3,2,1,0:T(8,128)}, u32[]{:S(2)}) copy-start(f32[4,8,2,8,2048]{4,3,2,1,0:T(8,128)} %spread.5) | copy-start | bytes 12582916
  323.6 47.0 %copy-start.5 = (f32[64,2048]{1,0:T(8,128)S(1)}, f32[64,2048]{1,0:T(8,128)}, u32[]{:S(2)}) copy-start(f32[64,2048]{1,0:T(8,128)} %get-tuple-element.30) | copy-start | bytes 1572868
Sparse Core Ops, SparseCore 0:
  11.8 59.6 all-gather.3
  79.4 52.1 reduce-scatter.3
  133.8 56.0 all-gather.5
  198.5 52.5 reduce-scatter.5
  253.3 56.0 all-gather.7
  318.1 52.4 reduce-scatter.7
